TPU v7x, 256 devices: a whole 4x4x8 slice. The times are simulated.
256 devices in a mesh: dp: 64 (over z_hi, x, y, core), fsdp: 4 (over z_lo).
Axes of the slice: x: 4, y: 4, z: 8 (z_hi: 2, z_lo: 4; z = z_hi * 4 + z_lo), core: 2. Of those that a mesh axis runs over, the one named last changes fastest.
Arguments:
- student_tiles: bfloat16 [32768, 16, 256], P(('dp', 'fsdp')), may hold values from -6 to 6
- teacher_tiles: bfloat16 [32768, 16, 512], P(('dp', 'fsdp')), may hold values from -6 to 6
- send_list: int32 [64, 4, 128], P('dp', 'fsdp'), may hold values from -1 to 127, as said below
- clip_weight: float32 [32768], P(('dp', 'fsdp')), may hold values from 0.5 to 64, as said below
- kernel_dilated: bfloat16 [1792, 256], P('fsdp'), may hold values from -0.125 to 0.125
- kernel_mix: bfloat16 [256, 256], P('fsdp'), may hold values from -0.375 to 0.375
- kernel_down: bfloat16 [4096, 512], P('fsdp'), may hold values from -0.09375 to 0.09375
- kernel_proj: bfloat16 [512, 1024], P('fsdp'), may hold values from -0.25 to 0.25
- kernel_teacher: bfloat16 [16, 512, 1024], P(None, 'fsdp'), may hold values from -0.0625 to 0.0625
- alpha_one: float32 [256], replicated, may hold values from 0.5 to 2
- alpha_two: float32 [256], replicated, may hold values from 0.5 to 2
- alpha_three: float32 [256], replicated, may hold values from 0.5 to 2
- alpha_teacher: float32 [512], replicated, may hold values from 0.5 to 2
Outputs:
- student_latent: bfloat16 [32768, 2, 1024], P(('dp', 'fsdp'))
- grad_dilated: float32 [458752], P(('dp', 'fsdp'))
- grad_mix: float32 [65536], P(('dp', 'fsdp'))
- grad_down: float32 [2097152], P(('dp', 'fsdp'))
- grad_proj: float32 [524288], P(('dp', 'fsdp'))
Inputs may be any that keep to these rules, and one draw needn't show every extreme that they name: `send_list`: entries d * 2 .. d * 2 + 1 of a device's list go to dp owner d. Each device's tiles 0 .. L - 1 appear exactly once and no other tile appears, for a count L of 2 to 128 drawn per device; on every device one owner receives 2 tiles, and some device has L = 128. `clip_weight`: positive weights.
All inputs are finite; a program needn't handle non-finite values.
Results may differ from a plain program's by a relative error of at most 0.0067.
Values may be sent and summed in bfloat16 or wider, within the bound.
A program may use at most 128 MiB of HBM per device.

v0:
```python
import jax
import jax.numpy as jnp
from jax import lax
from jax.sharding import PartitionSpec as P

DL = 1024
KS = 16
STRIDE = 8
DILATED_TAPS = 7
UNIT_DILATION = 3
TILE_FRAMES = 16
OUTF = 2


def snake(values, alpha_vec):
    widened = values.astype(jnp.float32)
    return widened + jnp.square(jnp.sin(alpha_vec * widened)) / alpha_vec


def snake_slope(values, alpha_vec):
    return 1.0 + jnp.sin(2.0 * alpha_vec * values)


def unfold_strided(frames):
    tile_count = frames.shape[0]
    margin = (KS - STRIDE) // 2
    padded_frames = jnp.pad(frames, ((0, 0), (margin, margin), (0, 0)))
    windows = [
        padded_frames[:, STRIDE * offset : STRIDE * offset + KS, :].reshape(tile_count, -1)
        for offset in range(OUTF)
    ]
    return jnp.stack(windows, axis=1)


def fold_strided(columns, channels):
    tile_count = columns.shape[0]
    margin = (KS - STRIDE) // 2
    padded_len = TILE_FRAMES + 2 * margin
    pieces = columns.reshape(tile_count, OUTF, KS, channels)
    folded = jnp.zeros((tile_count, padded_len, channels), jnp.float32)
    for offset in range(OUTF):
        folded = folded + jnp.pad(
            pieces[:, offset],
            ((0, 0), (STRIDE * offset, padded_len - KS - STRIDE * offset), (0, 0)),
        )
    return folded[:, margin : margin + TILE_FRAMES, :]


def unfold_dilated(frames):
    tile_count = frames.shape[0]
    receptive_length = UNIT_DILATION * (DILATED_TAPS - 1) // 2
    padded_frames = jnp.pad(frames, ((0, 0), (receptive_length, receptive_length), (0, 0)))
    tap_offsets = [
        padded_frames[
            :, UNIT_DILATION * tap_position : UNIT_DILATION * tap_position + TILE_FRAMES, :
        ]
        for tap_position in range(DILATED_TAPS)
    ]
    return jnp.stack(tap_offsets, axis=2).reshape(tile_count * TILE_FRAMES, -1)


def teacher_forward(tiles, kernel_teacher, alpha_teacher):
    tile_count = tiles.shape[0]
    activated = snake(tiles, alpha_teacher).astype(jnp.bfloat16)
    spread = lax.all_to_all(activated, "fsdp", split_axis=2, concat_axis=0, tiled=True)
    flat_kernel = kernel_teacher.reshape(-1, DL)
    columns = unfold_strided(spread).reshape(tile_count * lax.axis_size("fsdp") * OUTF, -1)
    return lax.psum_scatter(
        jnp.dot(columns, flat_kernel, preferred_element_type=jnp.float32).reshape(
            tile_count * lax.axis_size("fsdp"), OUTF, DL
        ),
        "fsdp",
        scatter_dimension=0,
        tiled=True,
    ).astype(jnp.bfloat16)


def student_step(tiles, target, weights, kernels, alphas):
    kernel_dilated, kernel_mix, kernel_down, kernel_proj = kernels
    alpha_one, alpha_two, alpha_three = alphas
    tile_count = tiles.shape[0]
    channels = tiles.shape[2]
    act_one = snake(tiles, alpha_one).astype(jnp.bfloat16)
    dilated = unfold_dilated(act_one)
    hidden = jnp.dot(dilated, kernel_dilated, preferred_element_type=jnp.float32)
    act_two = snake(hidden, alpha_two).astype(jnp.bfloat16)
    residual = tiles.reshape(tile_count * TILE_FRAMES, channels).astype(jnp.float32) + jnp.dot(
        act_two, kernel_mix, preferred_element_type=jnp.float32
    )
    act_three = (
        snake(residual, alpha_three).astype(jnp.bfloat16).reshape(tile_count, TILE_FRAMES, channels)
    )
    strided = unfold_strided(act_three).reshape(tile_count * OUTF, -1)
    student = jnp.dot(strided, kernel_down, preferred_element_type=jnp.float32).astype(jnp.bfloat16)
    predicted = jnp.dot(student, kernel_proj, preferred_element_type=jnp.float32)
    row_weight = jnp.repeat(weights, OUTF)[:, None]
    error = (
        row_weight
        * (predicted - target.reshape(tile_count * OUTF, DL).astype(jnp.float32))
        / (tile_count * OUTF)
    ).astype(jnp.bfloat16)
    grad_proj = jnp.dot(student.T, error, preferred_element_type=jnp.float32)
    back_student = jnp.dot(error, kernel_proj.T, preferred_element_type=jnp.float32).astype(
        jnp.bfloat16
    )
    grad_down = jnp.dot(strided.T, back_student, preferred_element_type=jnp.float32)
    back_columns = jnp.dot(back_student, kernel_down.T, preferred_element_type=jnp.float32).reshape(
        tile_count, OUTF, -1
    )
    back_three = fold_strided(back_columns, channels).reshape(tile_count * TILE_FRAMES, channels)
    back_residual = (back_three * snake_slope(residual, alpha_three)).astype(jnp.bfloat16)
    grad_mix = jnp.dot(act_two.T, back_residual, preferred_element_type=jnp.float32)
    back_hidden = (
        jnp.dot(back_residual, kernel_mix.T, preferred_element_type=jnp.float32)
        * snake_slope(hidden, alpha_two)
    ).astype(jnp.bfloat16)
    grad_dilated = jnp.dot(dilated.T, back_hidden, preferred_element_type=jnp.float32)
    latent = predicted.astype(jnp.bfloat16).reshape(tile_count, OUTF, DL)
    return (
        latent,
        (
            grad_dilated.reshape(-1),
            grad_mix.reshape(-1),
            grad_down.reshape(-1),
            grad_proj.reshape(-1),
        ),
    )


def on_device(
    student_tiles,
    teacher_tiles,
    send_list,
    clip_weight,
    kernel_dilated,
    kernel_mix,
    kernel_down,
    kernel_proj,
    kernel_teacher,
    alpha_one,
    alpha_two,
    alpha_three,
    alpha_teacher,
):
    routes = send_list.reshape(-1)
    live_rows = (routes >= 0)[:, None, None]
    picked = jnp.maximum(routes, 0)

    def packed(values):
        return jnp.where(live_rows, jnp.take(values, picked, axis=0), jnp.zeros((), values.dtype))

    student_part, teacher_part = (
        lax.all_to_all(packed(student_tiles), "dp", split_axis=0, concat_axis=0, tiled=True),
        lax.all_to_all(packed(teacher_tiles), "dp", split_axis=0, concat_axis=0, tiled=True),
    )
    target = teacher_forward(teacher_part, kernel_teacher, alpha_teacher)
    kernels = (
        lax.all_gather(kernel_dilated, "fsdp", axis=0, tiled=True),
        lax.all_gather(kernel_mix, "fsdp", axis=0, tiled=True),
        lax.all_gather(kernel_down, "fsdp", axis=0, tiled=True),
        lax.all_gather(kernel_proj, "fsdp", axis=0, tiled=True),
    )
    latent, gradients = student_step(
        student_part, target, clip_weight, kernels, (alpha_one, alpha_two, alpha_three)
    )
    gradients = (
        lax.psum_scatter(gradients[0], ("dp", "fsdp"), scatter_dimension=0, tiled=True),
        lax.psum_scatter(gradients[1], ("dp", "fsdp"), scatter_dimension=0, tiled=True),
        lax.psum_scatter(gradients[2], ("dp", "fsdp"), scatter_dimension=0, tiled=True),
        lax.psum_scatter(gradients[3], ("dp", "fsdp"), scatter_dimension=0, tiled=True),
    )
    return (latent, gradients[0], gradients[1], gradients[2], gradients[3])


def solution(mesh):
    placed = (
        P(("dp", "fsdp"), None, None),
        P(("dp", "fsdp"), None, None),
        P("dp", "fsdp", None),
        P(("dp", "fsdp")),
        P("fsdp", None),
        P("fsdp", None),
        P("fsdp", None),
        P("fsdp", None),
        P(None, "fsdp", None),
        P(),
        P(),
        P(),
        P(),
    )
    return jax.shard_map(
        on_device,
        mesh=mesh,
        in_specs=placed,
        out_specs=(
            P(("dp", "fsdp"), None, None),
            P(("dp", "fsdp")),
            P(("dp", "fsdp")),
            P(("dp", "fsdp")),
            P(("dp", "fsdp")),
        ),
        check_vma=False,
    )
```

profile of v0, /device:TPU:8, one launch (start us, length us, event | category | flops | bytes accessed | tf_op | source)
XLA Modules:
  0.0 759.4 jit_solution(11630443974876374161)
XLA Ops:
  8.8 2.0 gather_fusion.1
  10.8 3.0 select_select_fusion
  13.8 14.7 %all-to-all-start.1 = ((bf16[128,16,512]{2,1,0:T(8,128)(2,1)}), bf16[128,16,512]{2,1,0:T(8,128)(2,1)S(1)}, u32[]{:S(2)}, u32[]{:S(2)}) async-start(bf16[128,16,512]{2,1,0:T(8,128)(2,1)} %select_select_fusion), calls=%async_computation.1 | async-start | bytes 4194304 | tf_op jit(solution)/shard_map/all_to_all | solution.py:154
  29.3 46.7 %all-to-all-done.1 = bf16[128,16,512]{2,1,0:T(8,128)(2,1)S(1)} async-done(((bf16[128,16,512]{2,1,0:T(8,128)(2,1)}), bf16[128,16,512]{2,1,0:T(8,128)(2,1)S(1)}, u32[]{:S(2)}, u32[]{:S(2)}) %all-to-all-start.1) | async-done | bytes 2097184 | tf_op jit(solution)/shard_map/all_to_all | solution.py:154
  75.9 15.0 %fusion.3 = bf16[128,16,512]{2,1,0:T(8,128)(2,1)} fusion(bf16[128,16,512]{2,1,0:T(8,128)(2,1)S(1)} %all-to-all-done.1, f32[512]{0:T(512)S(1)} %copy-done.13), kind=kLoop, calls=%fused_computation.13 | loop fusion | flops 6291456 | bytes 4196352 | tf_op jit(solution)/shard_map/convert_element_type | solution.py:64
  91.0 4.2 copy.52
  95.2 93.7 %all_to_all.28 = bf16[128,16,512]{0,1,2:T(8,128)(2,1)} all-to-all(bf16[128,16,512]{0,1,2:T(8,128)(2,1)S(1)} %copy.52), channel_id=1, replica_groups=mesh['dp'=64,'fsdp'=4] {'fsdp'}, dimensions={2} | all-to-all | bytes 4194304 | tf_op jit(solution)/shard_map/all_to_all | solution.py:65
  189.0 5.1 copy.53
  194.0 5.3 pad_slice_fusion.7
  199.4 4.1 stack_reshape.15
  203.5 2.3 stack_reshape.14
  205.8 10.0 %fusion.4 = f32[512,2,1024]{2,0,1:T(8,128)} fusion(bf16[2048,1024,1]{1,0,2:T(8,128)(2,1)} %bitcast.109, bf16[512,1,2048]{2,0,1:T(8,128)(2,1)} %stack_reshape.15, bf16[512,1,2048]{2,0,1:T(8,128)(2,1)} %stack_reshape.14), kind=kOutput, calls=%fused_computation.14 | convolution fusion | flops 4297064448 | bytes 12582912 | tf_op jit(solution)/shard_map/dot_general | solution.py:69
  219.2 11.7 %all-to-all-start = ((bf16[128,16,256]{2,1,0:T(8,128)(2,1)}), bf16[128,16,256]{2,1,0:T(8,128)(2,1)S(1)}, u32[]{:S(2)}, u32[]{:S(2)}) async-start(bf16[128,16,256]{2,1,0:T(8,128)(2,1)} %select_select_fusion.1), calls=%async_computation | async-start | bytes 2097152 | tf_op jit(solution)/shard_map/all_to_all | solution.py:153
  232.0 56.0 %all_gather.13 = bf16[256,256]{1,0:T(8,128)(2,1)S(1)} all-gather(bf16[64,256]{1,0:T(8,128)(2,1)S(1)} %copy-done.11), channel_id=1, replica_groups=mesh['dp'=64,'fsdp'=4] {'fsdp'}, dimensions={0}, use_global_device_ids=true | all-gather | bytes 163840 | tf_op jit(solution)/shard_map/all_gather | solution.py:159
  288.0 34.1 %all_gather.12 = bf16[1792,256]{1,0:T(8,128)(2,1)} all-gather(bf16[448,256]{1,0:T(8,128)(2,1)S(1)} %copy-done.10), channel_id=1, replica_groups=mesh['dp'=64,'fsdp'=4] {'fsdp'}, dimensions={0}, use_global_device_ids=true | all-gather | bytes 1146880 | tf_op jit(solution)/shard_map/all_gather | solution.py:158
  322.1 7.3 add_convert_fusion.2
  333.4 7.9 %bitcast_dynamic-update-slice_fusion = bf16[128,16,7,256]{3,1,0,2:T(8,128)(2,1)} fusion(bf16[128,16,7,256]{3,1,0,2:T(8,128)(2,1)} %fusion.15, f32[256]{0:T(256)S(1)} %copy-done.12, bf16[128,16,256]{2,1,0:T(8,128)(2,1)S(1)} %all-to-all-done), kind=kLoop, calls=%fused_computation.53 | loop fusion | flops 3145728 | bytes 2098176
  345.3 14.4 %copy.49 = bf16[128,16,7,256]{3,2,1,0:T(8,128)(2,1)} copy(bf16[128,16,7,256]{3,1,0,2:T(8,128)(2,1)} %fusion.21) | data formatting | bytes 14680064 | tf_op jit(solution)/shard_map/stack | solution.py:59
  359.8 7.2 copy.59
  367.0 2.1 fusion.26
  369.9 15.2 %add_convert_fusion = (bf16[2048,256]{1,0:T(8,128)(2,1)S(1)}, f32[2048,256]{1,0:T(8,128)}) fusion(f32[256]{0:T(256)S(1)} %copy-done.14, bf16[256,256]{1,0:T(8,128)(2,1)S(1)} %all_gather.13, f32[2048,256]{1,0:T(8,128)S(1)} %fusion.26, f32[256]{0:T(256)S(1)} %copy-done.15, bf16[2048,256]{1,0:T(8,128)(2,1)S(1)} %bitcast.98), kind=kOutput, calls=%fused_computation.31 | convolution fusion | flops 274726912 | bytes 6424576 | tf_op jit(solution)/shard_map/dot_general | solution.py:87
  386.6 4.0 copy.51
  390.6 2.9 reshape.89
  393.5 3.4 convolution_convert_fusion.1
  402.1 2.5 multiply_convert_fusion
  406.9 4.5 convolution_bitcast_fusion
  416.6 7.2 fusion.9
  423.8 7.6 %convolution_bitcast_fusion.3 = f32[32,2,8,128]{3,2,1,0:T(8,128)S(1)} fusion(bf16[2048,256]{1,0:T(8,128)(2,1)S(1)} %fusion.9, f32[2048,256]{1,0:T(8,128)S(1)} %copy-done.18, f32[256]{0:T(256)S(1)} %copy-done.15), kind=kOutput, calls=%fused_computation.40 | convolution fusion | flops 271056896 | bytes 3408896 | tf_op jit(solution)/shard_map/dot_general | solution.py:112
  431.5 12.2 %convolution_bitcast_fusion.2 = f32[224,2,8,128]{3,2,1,0:T(8,128)S(1)} fusion(bf16[2048,1792]{1,0:T(8,128)(2,1)} %bitcast.104, bf16[2048,256]{1,0:T(8,128)(2,1)S(1)} %fusion.9, bf16[256,256]{1,0:T(8,128)(2,1)S(1)} %all_gather.13, f32[2048,256]{1,0:T(8,128)} %copy-done.17, f32[256]{0:T(256)S(1)} %broadcast_multiply_fusion), kind=kOutput, calls=%fused_computation.37 | convolution fusion | flops 2149580800 | bytes 12452864 | tf_op jit(solution)/shard_map/dot_general | solution.py:117
  443.7 2.2 copy.61
  446.7 9.0 %copy.63 = f32[512,4,8,128]{3,1,2,0:T(4,128)} copy(f32[512,4,8,128]{3,2,1,0:T(8,128)} %convolution_bitcast_fusion) | data formatting | bytes 16777216
  459.5 287.5 %all-reduce.12.cloned.1.call-done = (f32[458752]{0:T(1024)}, f32[65536]{0:T(1024)}, f32[2097152]{0:T(1024)}, f32[524288]{0:T(1024)}) async-done(((f32[458752]{0:T(1024)}, f32[65536]{0:T(1024)}, f32[2097152]{0:T(1024)}, f32[524288]{0:T(1024)}), (f32[458752]{0:T(1024)}, f32[65536]{0:T(1024)}, f32[2097152]{0:T(1024)}, f32[524288]{0:T(1024)})) %all-reduce.12.cloned.1.call-update) | async-done | bytes 12582928
  (84 shorter events, 39.8 us)
Async XLA Ops:
  7.2 1.6 copy-start
  13.8 62.2 %copy-start.13 = (f32[512]{0:T(512)S(1)}, f32[512]{0:T(512)}, u32[]{:S(2)}) copy-start(f32[512]{0:T(512)} %param.25) | copy-start | bytes 6148
  13.8 62.2 %all-to-all-start.1 = ((bf16[128,16,512]{2,1,0:T(8,128)(2,1)}), bf16[128,16,512]{2,1,0:T(8,128)(2,1)S(1)}, u32[]{:S(2)}, u32[]{:S(2)}) async-start(bf16[128,16,512]{2,1,0:T(8,128)(2,1)} %select_select_fusion), calls=%async_computation.1 | async-start | bytes 4194304 | tf_op jit(solution)/shard_map/all_to_all | solution.py:154
  28.5 365.0 %all-gather.3.cloned.1.call-start = ((), (), s32[]{:S(2)}) async-start(), calls=%async_computation.4 | async-start | bytes 5242880 | tf_op jit(solution)/shard_map/all_gather | solution.py:160
  29.2 367.8 %reduce-scatter.2.cloned.1.call-start = ((), (), s32[]{:S(2)}) async-start(), calls=%async_computation.6 | async-start | bytes 5242880 | tf_op jit(solution)/shard_map/reduce_scatter | solution.py:68
  215.8 1.2 copy-start.8
  217.7 14.1 %copy-start.16 = (f32[128]{0:T(128)S(1)}, f32[128]{0:T(128)}, u32[]{:S(2)}) copy-start(f32[128]{0:T(128)} %param.16) | copy-start | bytes 1540
  217.7 14.3 %copy-start.11 = (bf16[64,256]{1,0:T(8,128)(2,1)S(1)}, bf16[64,256]{1,0:T(8,128)(2,1)}, u32[]{:S(2)}) copy-start(bf16[64,256]{1,0:T(8,128)(2,1)} %param.18) | copy-start | bytes 98308
  217.7 70.3 %copy-start.14 = (f32[256]{0:T(256)S(1)}, f32[256]{0:T(256)}, u32[]{:S(2)}) copy-start(f32[256]{0:T(256)} %param.24) | copy-start | bytes 3076
  217.7 70.3 %copy-start.15 = (f32[256]{0:T(256)S(1)}, f32[256]{0:T(256)}, u32[]{:S(2)}) copy-start(f32[256]{0:T(256)} %param.23) | copy-start | bytes 3076
  217.7 70.3 %copy-start.10 = (bf16[448,256]{1,0:T(8,128)(2,1)S(1)}, bf16[448,256]{1,0:T(8,128)(2,1)}, u32[]{:S(2)}) copy-start(bf16[448,256]{1,0:T(8,128)(2,1)} %param.17) | copy-start | bytes 688132
  219.2 102.9 %copy-start.12 = (f32[256]{0:T(256)S(1)}, f32[256]{0:T(256)}, u32[]{:S(2)}) copy-start(f32[256]{0:T(256)} %param.22) | copy-start | bytes 3076
  219.2 102.8 %all-to-all-start = ((bf16[128,16,256]{2,1,0:T(8,128)(2,1)}), bf16[128,16,256]{2,1,0:T(8,128)(2,1)S(1)}, u32[]{:S(2)}, u32[]{:S(2)}) async-start(bf16[128,16,256]{2,1,0:T(8,128)(2,1)} %select_select_fusion.1), calls=%async_computation | async-start | bytes 2097152 | tf_op jit(solution)/shard_map/all_to_all | solution.py:153
  230.9 171.1 %all-gather.5.cloned.1.call-start = ((), (), s32[]{:S(2)}) async-start(), calls=%async_computation.5 | async-start | bytes 1310720 | tf_op jit(solution)/shard_map/all_gather | solution.py:161
  231.7 515.4 %all-reduce.12.cloned.1.call-start = ((), (), s32[]{:S(2)}) async-start(), calls=%async_computation.7 | async-start | bytes 25165824
  359.8 7.2 copy-start.9
  366.9 2.9 copy-start.3
  369.9 15.2 %copy-start.17 = (f32[2048,256]{1,0:T(8,128)}, f32[2048,256]{1,0:T(8,128)S(1)}, u32[]{:S(2)}) copy-start(f32[2048,256]{1,0:T(8,128)S(1)} %fusion.26) | copy-start | bytes 6291460
  404.6 1.8 copy-start.4
  406.9 4.6 copy-start.5
  415.0 1.6 copy-start.7
  416.6 7.2 copy-start.18
  446.7 9.0 %copy-start.2 = (f32[64,8,8,128]{3,2,1,0:T(8,128)S(1)}, f32[64,8,8,128]{3,2,1,0:T(8,128)}, u32[]{:S(2)}) copy-start(f32[64,8,8,128]{3,2,1,0:T(8,128)} %convolution_bitcast_fusion.1) | copy-start | bytes 6291460
  457.5 1.0 copy-start.6
  457.5 294.9 %copy-start.1 = (bf16[128,16,512]{2,1,0:T(8,128)(2,1)S(1)}, bf16[128,16,512]{2,1,0:T(8,128)(2,1)}, u32[]{:S(2)}) copy-start(bf16[128,16,512]{2,1,0:T(8,128)(2,1)} %param.14) | copy-start | bytes 6291460
Sparse Core Ops, SparseCore 0:
  31.1 111.8 all-gather.2
  215.9 121.1 reduce-scatter.1
  339.0 33.9 all-gather.4
  457.7 289.3 all-reduce.11
where the time goes:
time: 769 us; the launch traced here: 759 us
  waiting for transfers between devices  336 us (44%)
  blocking collectives  184 us (24%)
  local copies, waits for them, and re-layouts  92.4 us (12%)
  matrix products  61.1 us (8%)
  other arithmetic  45.3 us (6%)
  starting transfers between devices  26.6 us (3%)
  between operations  14.5 us (2%)
    unnamed x5, waiting for transfers between devices  289 us
    all_to_all x1, blocking collectives, teacher_forward(): lax.all_to_all(activated, 'fsdp', split_axis=2, concat_axis=0, tiled=True)  93.7 us
    all_gather x1, blocking collectives, on_device(): lax.all_gather(kernel_mix, 'fsdp', axis=0, tiled=True)  56 us
    all_to_all x1, waiting for transfers between devices, on_device(): lax.all_to_all(packed(teacher_tiles), 'dp', split_axis=0, concat_axis=0,...  46.7 us
    unnamed x53, local copies, waits for them, and re-layouts  39.3 us
    all_gather x1, blocking collectives, on_device(): lax.all_gather(kernel_dilated, 'fsdp', axis=0, tiled=True)  34.1 us
    another operation x2, local copies, waits for them, and re-layouts, unfold_dilated(): return jnp.stack(tap_offsets, axis=2).reshape(tile_count * TILE_FRAMES, -1)  15.6 us
  transfers between devices with their start and end apart: 6, of which 2 were waited for; matrix products, arithmetic and copies ran while one was open for 17% of the time, Pallas kernels for 0%

commit v1 on v0

v1 whole, which is shorter than its diff:
```python
import jax
import jax.numpy as jnp
import numpy as np
from jax import lax
from jax.experimental import pallas as pl
from jax.experimental.pallas import tpu as pltpu
from jax.sharding import PartitionSpec as P

BF = jnp.bfloat16
F32 = jnp.float32
MESH = pl.DeviceIdType.MESH
VMEM_LIMIT = 66_000_000


def dot(a, b):
    return jnp.dot(a, b, preferred_element_type=F32)


def dot_bt(a, b):
    return lax.dot_general(a, b, (((1,), (1,)), ((), ())), preferred_element_type=F32)


PI_PARTS = (3.125, 0.015625, 9.67502593994140625e-4, 1.509957990978376432e-7)


def fit_sin_cos():
    nodes = np.cos(np.pi * (np.arange(400) + 0.5) / 400)
    u = (nodes + 1) * 0.5 * (np.pi / 2 * 1.002) ** 2
    r = np.sqrt(u)
    sin_c = np.polynomial.polynomial.polyfit(u, np.sin(r) / r, 5)
    cos_c = np.polynomial.polynomial.polyfit(u, np.cos(r), 5)
    return [float(c) for c in sin_c], [float(c) for c in cos_c]


SIN_C, COS_C = fit_sin_cos()


def horner(u, coefs):
    acc = jnp.full_like(u, coefs[-1])
    for c in coefs[-2::-1]:
        acc = acc * u + c
    return acc


def reduce_pi(y):
    n = jnp.round(y * (1.0 / np.pi))
    r = y
    for part in PI_PARTS:
        r = r - n * part
    return r


def snake_only(v, alpha, inv):
    r = reduce_pi(alpha * v)
    s = r * horner(r * r, SIN_C)
    return v + s * s * inv


def snake_slope(v, alpha, inv):
    r = reduce_pi(alpha * v)
    u = r * r
    s = r * horner(u, SIN_C)
    c = horner(u, COS_C)
    return v + s * s * inv, 1.0 + 2.0 * s * c


def coords():
    d = lax.axis_index("dp")
    f = lax.axis_index("fsdp")
    core = d % 2
    y = (d // 2) % 4
    x = (d // 8) % 4
    zhi = d // 32
    return d, f, zhi, x, y, core


def dp_of(zhi, x, y, core):
    return ((zhi * 4 + x) * 4 + y) * 2 + core


def z_peer(zhi, f, step):
    z = (zhi * 4 + f + step + 8) % 8
    return z // 4, z % 4


class Batch:
    def __init__(self, send, recv):
        self.send, self.recv, self.next = send, recv, 0
        self.all = []

    def start(self, src, dst, device):
        copy = pltpu.make_async_remote_copy(
            src_ref=src,
            dst_ref=dst,
            send_sem=self.send.at[self.next],
            recv_sem=self.recv.at[self.next],
            device_id=device,
            device_id_type=MESH,
        )
        self.next += 1
        copy.start()
        self.all.append(copy)
        return copy

    def finish(self):
        for copy in self.all:
            copy.wait_send()


def greet(peers):
    barrier = pltpu.get_barrier_semaphore()
    for peer in peers:
        pl.semaphore_signal(barrier, inc=1, device_id=peer, device_id_type=MESH)
    pl.semaphore_wait(barrier, len(peers))


CHUNKS = 2
N_GATHER = 400


def gather_kernel(
    teach, down, proj, dil, mix, cw,
    teach_g, down_g, proj_g, dil_g, mix_g, cw_g,
    stage_t, stage_d, stage_p, stage_l, stage_m, stage_c, local_in, local_out, send, recv,
):
    d, f, zhi, x, y, core = coords()
    partner = (dp_of(zhi, x, y, 1 - core), f)
    x_peers = [(dp_of(zhi, (x + k) % 4, y, core), f) for k in (1, 2, 3)]
    y_peers = [(dp_of(zhi, x, (y + k) % 4, core), f) for k in (1, 2, 3)]
    up_h, up_f = z_peer(zhi, f, 1)
    dn_h, dn_f = z_peer(zhi, f, -1)
    far_h, far_f = z_peer(zhi, f, 2 - 4 * core)
    far2_h, far2_f = z_peer(zhi, f, 4 * core - 2)
    z_peers = [
        (dp_of(up_h, x, y, core), up_f),
        (dp_of(dn_h, x, y, core), dn_f),
        (dp_of(far_h, x, y, core), far_f),
    ]
    other = (dp_of(1 - zhi, x, y, core), f)
    remote = [(f + r) % 4 for r in (1, 2, 3)]
    own = [(teach, stage_t), (down, stage_d), (proj, stage_p), (dil, stage_l), (mix, stage_m), (cw, stage_c)]
    outs = [teach_g.at[f], down_g.at[f], proj_g.at[f], dil_g.at[f], mix_g.at[f], cw_g.at[zhi, x, y, core]]
    loads = []
    for i, (src, stage) in enumerate(own):
        loads.append(pltpu.make_async_copy(src, stage, local_in.at[i]))
        loads[-1].start()
    greet(z_peers + [(dp_of(far2_h, x, y, core), far2_f), other, partner] + x_peers + y_peers)
    b = Batch(send, recv)
    cw_z = b.start(cw, cw_g.at[zhi, x, y, core], other)

    @pl.when(core == 0)
    def _():
        pass

    chunks = [("d", None)] + [("t", c) for c in range(CHUNKS)]

    def src_piece(chunk):
        kind, c = chunk
        return down.at[x, y, core] if kind == "d" else teach.at[x, y, core, :, c]

    def piece(chunk, shard, xs, ys, cs, half):
        kind, c = chunk
        if kind == "d":
            return down_g.at[shard, xs, ys, cs, half]
        return teach_g.at[shard, xs, ys, cs, half, c]

    every = slice(None)
    z_wait = []
    for chunk in chunks:
        z_wait.append([b.start(src_piece(chunk), piece(chunk, f, x, y, core, every), peer) for peer in z_peers])
        if chunk[0] == "d":
            small = []
            for peer in z_peers:
                small.append(b.start(proj.at[core], proj_g.at[f, core], peer))
                small.append(b.start(dil.at[core], dil_g.at[f, core], peer))
                small.append(b.start(mix.at[core], mix_g.at[f, core], peer))
    to_partner = []
    cw_wait = []
    s1_wait = []
    for i, chunk in enumerate(chunks):
        for copy in z_wait[i]:
            copy.wait_recv()
        here = [[], []]
        for shard in remote:
            mine = [piece(chunk, shard, x, y, core, h) for h in (0, 1)]
            for k in range(3):
                here[0].append(b.start(mine[0], mine[0], x_peers[k]))
                here[1].append(b.start(mine[1], mine[1], y_peers[k]))
            whole = piece(chunk, shard, x, y, core, every)
            to_partner.append(b.start(whole, whole, partner))
        s1_wait.append(here)
        if i == 0:
            cw_z.wait_recv()
            line = cw_g.at[1 - zhi, x, y, core]
            cw_wait = [b.start(cw, cw_g.at[zhi, x, y, core], peer) for peer in x_peers]
            cw_wait += [b.start(line, line, peer) for peer in x_peers]
            for copy in small:
                copy.wait_recv()
            for shard in remote:
                to_partner.append(b.start(proj_g.at[shard, core], proj_g.at[shard, core], partner))
                to_partner.append(b.start(dil_g.at[shard, core], dil_g.at[shard, core], partner))
                to_partner.append(b.start(mix_g.at[shard, core], mix_g.at[shard, core], partner))
    stores = []
    for i, (src, stage) in enumerate(own):
        loads[i].wait()
        stores.append(pltpu.make_async_copy(stage, outs[i], local_out.at[i]))
        stores[-1].start()
    stores[5].wait()
    s2_wait = []
    for i, chunk in enumerate(chunks):
        here = [[], []]
        for h in (0, 1):
            for copy in s1_wait[i][h]:
                copy.wait_recv()
            for shard in remote:
                if h == 0:
                    block = piece(chunk, shard, every, y, core, 0)
                else:
                    block = piece(chunk, shard, x, every, core, 1)
                for k in range(3):
                    here[h].append(b.start(block, block, (y_peers if h == 0 else x_peers)[k]))
                for k in range(1, 4):
                    if h == 0:
                        one = piece(chunk, shard, (x + k) % 4, y, core, 0)
                    else:
                        one = piece(chunk, shard, x, (y + k) % 4, core, 1)
                    to_partner.append(b.start(one, one, partner))
        s2_wait.append(here)
        if i == 0:
            for copy in cw_wait:
                copy.wait_recv()
            block = cw_g.at[:, :, y, core]
            cw_wait = [b.start(block, block, peer) for peer in y_peers]
    for i, chunk in enumerate(chunks):
        for h in (0, 1):
            for copy in s2_wait[i][h]:
                copy.wait_recv()
            for shard in remote:
                for k in range(1, 4):
                    if h == 0:
                        one = piece(chunk, shard, every, (y + k) % 4, core, 0)
                    else:
                        one = piece(chunk, shard, (x + k) % 4, every, core, 1)
                    to_partner.append(b.start(one, one, partner))
        if i == 0:
            for copy in cw_wait:
                copy.wait_recv()
            block = cw_g.at[:, :, :, core]
            to_partner.append(b.start(block, block, partner))
    for copy in to_partner:
        copy.wait_recv()
    for copy in stores[:5]:
        copy.wait()
    b.finish()


def gather_kernels(kernel_teacher, kernel_down, kernel_proj, kernel_dilated, kernel_mix, clip_weight):
    rows = 32 // CHUNKS
    shapes = [(4, 4, 2, 2, CHUNKS, rows, 1024), (4, 4, 2, 2, 16, 512), (2, 64, 1024), (2, 224, 256), (2, 32, 256)]
    args = [
        value.reshape(shape)
        for value, shape in zip((kernel_teacher, kernel_down, kernel_proj, kernel_dilated, kernel_mix), shapes)
    ]
    cw = clip_weight.reshape(1, 128)
    outs = [jax.ShapeDtypeStruct((4,) + shape, BF) for shape in shapes]
    outs.append(jax.ShapeDtypeStruct((2, 4, 4, 2, 1, 128), F32))
    anywhere = pl.BlockSpec(memory_space=pl.ANY)
    return pl.pallas_call(
        gather_kernel,
        out_shape=outs,
        in_specs=[anywhere] * 6,
        out_specs=[anywhere] * 6,
        scratch_shapes=[pltpu.VMEM(shape, BF) for shape in shapes]
        + [
            pltpu.VMEM((1, 128), F32),
            pltpu.SemaphoreType.DMA((6,)),
            pltpu.SemaphoreType.DMA((6,)),
            pltpu.SemaphoreType.DMA((N_GATHER,)),
            pltpu.SemaphoreType.DMA((N_GATHER,)),
        ],
        compiler_params=pltpu.CompilerParams(collective_id=0, has_side_effects=True, vmem_limit_bytes=VMEM_LIMIT),
        name="gather_kernels",
    )(*args, cw)


GROUPS = ((0, 3), (3, 3), (6, 1), (7, 2), (9, 1), (10, 3), (13, 3))


def permutations():
    out = np.arange(256)
    tile = np.zeros((256, 256), np.float32)
    tile[out, (out % 16) * 16 + out // 16] = 1
    proj = np.zeros((256, 256), np.float32)
    block, m = out // 16, out % 16
    proj[out, (m % 8) * 32 + block * 2 + m // 8] = 1
    dil = np.zeros((256, 256), np.float32)
    dil[out, np.where(m < 14, (m % 2) * 112 + block * 7 + m // 2, 224 + (m - 14) * 16 + block)] = 1
    out = np.arange(512)
    lat = np.zeros((512, 512), np.float32)
    lat[out, (out % 32) * 16 + out // 32] = 1
    return [jnp.asarray(p, BF) for p in (tile, proj, dil, lat)]


def step_kernel(
    routes, weight, xs, xt, teach, down, proj, dil, mix, a1, a2, a3, at, p_tile, p_proj, p_dil, p_lat,
    lat_out, grads,
    w_t, x1s, x1t, act1, act1t, act2t, act3, act3t, act_t, hid, slope3, target, pred, error, back3, back_h, back_r,
    g_dil, stud, sems,
):
    taps = [(k if k < 16 else None) for k in (4, 5, 6, 7, 8, 9, 10, 11, 0, 12, 1, 13, 2, 14, 3, 15)]

    def tap_copy(k):
        return pltpu.make_async_copy(teach.at[:, k], w_t.at[k], sems.at[k])

    for k in taps:
        tap_copy(k).start()

    def alphas(ref):
        a = ref[...]
        return a, 1.0 / a

    @pl.loop(0, 8)
    def _(g):
        rows = pl.ds(pl.multiple_of(g * 256, 256), 256)
        cols = pl.ds(pl.multiple_of(g * 16, 16), 16)
        x1s[:, cols, :] = dot(p_tile[...], xs[rows, :]).astype(BF).reshape(16, 16, 256)
        x1t[:, cols, :] = dot(p_tile[...], xt[rows, :]).astype(BF).reshape(16, 16, 512)

    pick = jnp.where(
        routes[...] == lax.broadcasted_iota(jnp.int32, (128, 128), 1), 1.0, 0.0
    ).astype(BF)

    @pl.loop(0, 16)
    def _(j):
        value = dot(pick, x1s[j])
        x1s[j] = value.astype(BF)
        one = snake_only(value, *alphas(a1))
        act1[j] = one.astype(BF)
        act1t[j] = one.T.astype(BF)
        teacher = snake_only(dot(pick, x1t[j]), *alphas(at))
        act_t[j] = teacher.astype(BF)

    for first, count in GROUPS:
        valid = [k for k in range(7) if 0 <= first + 3 * (k - 3) <= 15]
        lhs = jnp.concatenate(
            [act1[first + 3 * (k - 3) : first + 3 * (k - 3) + count].reshape(count * 128, 256) for k in valid], axis=1
        )
        hid[first : first + count] = dot(lhs, dil[valid[0] * 256 : (valid[-1] + 1) * 256, :]).reshape(count, 128, 256)

    @pl.loop(0, 16)
    def _(j):
        act, slope = snake_slope(hid[j], *alphas(a2))
        hid[j] = slope
        act2t[j] = act.T.astype(BF)
        residual = x1s[j].astype(F32) + dot(act.astype(BF), mix[...])
        act, slope = snake_slope(residual, *alphas(a3))
        slope3[j] = slope
        act3[j] = act.astype(BF)
        act3t[j] = act.T.astype(BF)

    lhs = jnp.concatenate([jnp.concatenate([act3[k - 4], act3[k + 4]], axis=0) for k in range(4, 12)], axis=1)
    both = dot(lhs, down[1024:3072, :])
    first = dot(jnp.concatenate([act3[k] for k in range(8, 12)], axis=1), down[3072:4096, :])
    second = dot(jnp.concatenate([act3[k] for k in range(4, 8)], axis=1), down[0:1024, :])
    stud[0:128, :] = (both[0:128] + first).astype(BF)
    stud[128:256, :] = (both[128:256] + second).astype(BF)
    pred[...] = dot(stud[...], proj[...])

    target[...] = jnp.zeros_like(target)

    @pl.loop(4, 12)
    def _(k):
        tap_copy(k).wait()
        lhs = jnp.concatenate([act_t[k - 4], act_t[k + 4]], axis=0)
        target[...] += dot(lhs, w_t[k].reshape(512, 1024))

    @pl.loop(0, 4)
    def _(k):
        tap_copy(k).wait()
        target[128:256, :] += dot(act_t[k + 4], w_t[k].reshape(512, 1024))
        tap_copy(k + 12).wait()
        target[0:128, :] += dot(act_t[k + 8], w_t[k + 12].reshape(512, 1024))

    error[...] = (weight[...] * (pred[...] - target[...].astype(BF).astype(F32)) / 256.0).astype(BF)

    @pl.loop(0, 4)
    def _(g):
        parts = [
            pred[pl.ds(pl.multiple_of(o * 128 + c * 64 + g * 16, 16), 16), cb * 128 : (cb + 1) * 128].astype(BF)
            for c in range(2)
            for o in range(2)
            for cb in range(8)
        ]
        moved = dot(p_lat[...], jnp.concatenate(parts, axis=0)).astype(BF)
        lat_out[pl.ds(g * 16, 16)] = moved.reshape(16, 32, 128)

    back_s = dot_bt(error[...], proj[...]).astype(BF)

    g_proj = dot(stud[...].astype(F32).T.astype(BF), error[...])
    target[...] = g_proj[0:256]
    pred[...] = g_proj[256:512]

    @pl.loop(0, 8)
    def _(g):
        rows = pl.ds(pl.multiple_of(g * 32, 32), 32)
        for base, ref in ((0, target), (128, pred)):
            stack = jnp.concatenate([ref[rows, cb * 128 : (cb + 1) * 128].astype(BF) for cb in range(8)], axis=0)
            moved = dot(p_proj[...], stack).astype(BF).reshape(16, 16, 128)
            grads[pl.ds(base + g * 16, 16), 80:96, :] = moved

    stud[...] = back_s

    def put_down(k, value):
        for cb in range(4):
            part = value[:, cb * 128 : (cb + 1) * 128].astype(BF).reshape(16, 16, 128)
            grads[pl.ds(k * 16, 16), cb * 16 : (cb + 1) * 16, :] = part

    def tap_rows(k):
        return down[pl.ds(pl.multiple_of(k * 256, 256), 256), :]

    @pl.loop(4, 12)
    def _(k):
        put_down(k, dot(jnp.concatenate([act3t[k - 4], act3t[k + 4]], axis=1), stud[...]))
        part = dot_bt(stud[...], tap_rows(k))
        back3[k - 4] = part[0:128]
        back3[k + 4] = part[128:256]

    @pl.loop(0, 4)
    def _(k):
        put_down(k, dot(act3t[k + 4], stud[128:256, :]))
        put_down(k + 12, dot(act3t[k + 8], stud[0:128, :]))
        back3[k + 4] += dot_bt(stud[128:256, :], tap_rows(k))
        back3[k + 8] += dot_bt(stud[0:128, :], tap_rows(k + 12))

    g_dil[1792:2048, :] = jnp.zeros((256, 256), F32)

    @pl.loop(0, 16)
    def _(j):
        back = (back3[j] * slope3[j]).astype(BF)
        g_dil[1792:2048, :] += dot(act2t[j], back)
        back_h[j] = (dot_bt(back, mix[...]) * hid[j]).astype(BF)

    for k in range(7):
        shift = 3 * (k - 3)
        low, high = max(0, -shift), min(16, 16 - shift)
        lhs = jnp.concatenate([act1t[j + shift] for j in range(low, high)], axis=1)
        g_dil[k * 256 : (k + 1) * 256, :] = dot(lhs, back_h[low:high].reshape((high - low) * 128, 256))

    @pl.loop(0, 16)
    def _(g):
        rows = pl.ds(pl.multiple_of(g * 112, 16), 112)
        more = pl.ds(pl.multiple_of(1792 + g * 16, 16), 16)
        stack = jnp.concatenate(
            [g_dil[rows, 0:128], g_dil[rows, 128:256], g_dil[more, 0:128], g_dil[more, 128:256]], axis=0
        ).astype(BF)
        grads[pl.ds(g * 16, 16), 64:80, :] = dot(p_dil[...], stack).astype(BF).reshape(16, 16, 128)


def local_step(routes, weight, xs, xt, gathered, alphas):
    teach, down, proj, dil, mix = gathered
    in_vmem = pl.BlockSpec(memory_space=pltpu.VMEM)
    anywhere = pl.BlockSpec(memory_space=pl.ANY)
    frames = lambda c, t: pltpu.VMEM((16, 128, c), t)
    turned = pltpu.VMEM((16, 256, 128), BF)
    return pl.pallas_call(
        step_kernel,
        out_shape=[jax.ShapeDtypeStruct((64, 32, 128), BF), jax.ShapeDtypeStruct((256, 96, 128), BF)],
        in_specs=[in_vmem] * 4 + [anywhere] + [in_vmem] * 12,
        out_specs=[in_vmem] * 2,
        scratch_shapes=[
            pltpu.VMEM((16, 4, 128, 1024), BF),
            frames(256, BF), frames(512, BF), frames(256, BF), turned, turned, frames(256, BF), turned,
            frames(512, BF), frames(256, F32), frames(256, F32),
            pltpu.VMEM((256, 1024), F32), pltpu.VMEM((256, 1024), F32), pltpu.VMEM((256, 1024), BF),
            frames(256, F32), frames(256, BF), pltpu.VMEM((8, 128), BF),
            pltpu.VMEM((2048, 256), F32), pltpu.VMEM((256, 512), BF), pltpu.SemaphoreType.DMA((16,)),
        ],
        compiler_params=pltpu.CompilerParams(vmem_limit_bytes=VMEM_LIMIT),
        name="local_step",
    )(routes, weight, xs, xt, teach, down, proj, dil, mix, *alphas, *permutations())


def exchange_kernel(
    lat, grads, lat_g, total,
    r0, s1, r1, s2, r2, s3, r3, lat_sem, own_sem, send, recv,
):
    d, f, zhi, x, y, core = coords()
    partner = (dp_of(zhi, x, y, 1 - core), f)
    x_peers = [(dp_of(zhi, (x + k) % 4, y, core), f) for k in (1, 2, 3)]
    y_peers = [(dp_of(zhi, x, (y + k) % 4, core), f) for k in (1, 2, 3)]
    z_ids = [z_peer(zhi, f, k) for k in range(1, 8)]
    z_peers = [(dp_of(h, x, y, core), g) for h, g in z_ids]
    barrier = pltpu.get_barrier_semaphore()

    def hello(k, carry):
        pl.semaphore_signal(barrier, inc=1, device_id=((d + k) % 64, f), device_id_type=MESH)
        return carry

    lax.fori_loop(1, 64, hello, 0)
    for k, peer in enumerate(z_peers):
        if k != 3:
            pl.semaphore_signal(barrier, inc=1, device_id=peer, device_id_type=MESH)
    pl.semaphore_wait(barrier, 63 + 6)

    own = pltpu.make_async_copy(lat.at[d], lat_g.at[d], own_sem)
    own.start()
    b = Batch(send, recv)
    pieces = [[], []]
    order = (1, 2, 3, 0)
    for k in order:
        for h in (0, 1):
            if h == 0:
                src = grads.at[:, (x + k) % 4, :, 1 - core, :, 0]
            else:
                src = grads.at[:, :, (y + k) % 4, 1 - core, :, 1]
            pieces[h].append(b.start(src, r0.at[h, k], partner))

    def lat_copy(k):
        to = (d + k) % 64
        return pltpu.make_async_remote_copy(
            src_ref=lat.at[to], dst_ref=lat_g.at[d], send_sem=lat_sem.at[0, k - 1], recv_sem=lat_sem.at[1, k - 1],
            device_id=(to, f), device_id_type=MESH,
        )

    first = [[], []]
    for i, k in enumerate(order):
        for h in (0, 1):
            pieces[h][i].wait_recv()

            @pl.loop(0, 8)
            def _(n):
                if h == 0:
                    mine = grads[n // 4, (x + k) % 4, n % 4, core, :, 0]
                else:
                    mine = grads[n // 4, n % 4, (y + k) % 4, core, :, 1]
                s1[h, k, n // 4, n % 4] = (mine.astype(F32) + r0[h, k, n // 4, n % 4].astype(F32)).astype(BF)

            if k > 0:
                first[h].append(b.start(s1.at[h, k], r1.at[h, k - 1], (x_peers, y_peers)[h][k - 1]))

    def send_lat(k, carry):
        lat_copy(k).start()
        return carry

    lax.fori_loop(1, 64, send_lat, 0)

    second = [[], []]
    for h in (0, 1):
        for copy in first[h]:
            copy.wait_recv()

        @pl.loop(0, 8)
        def _(n):
            a, e = n // 4, n % 4
            acc = s1[h, 0, a, e].astype(F32)
            for k in range(3):
                acc = acc + r1[h, k, a, e].astype(F32)
            s2[h, e, a] = acc.astype(BF)

        mine = (y, x)[h]
        for k in (1, 2, 3):
            second[h].append(b.start(s2.at[h, (mine + k) % 4], r2.at[h, k - 1], (y_peers, x_peers)[h][k - 1]))
    third = [[], []]
    for h in (0, 1):
        for copy in second[h]:
            copy.wait_recv()
        mine = (y, x)[h]

        @pl.loop(0, 2)
        def _(a):
            acc = s2[h, mine, a].astype(F32)
            for k in range(3):
                acc = acc + r2[h, k, a].astype(F32)
            s3[h, a] = acc.astype(BF)

        for k in range(7):
            zh, zf = z_ids[k]
            third[h].append(b.start(s3.at[h, zh, zf], r3.at[h, k], z_peers[k]))
    for h in (0, 1):
        for copy in third[h]:
            copy.wait_recv()
        acc = s3[h, zhi, f].astype(F32)
        for k in range(7):
            acc = acc + r3[h, k].astype(F32)
        total[h] = acc
    own.wait()

    def wait_lat(k, carry):
        copy = lat_copy(k)
        copy.wait_recv()
        copy.wait_send()
        return carry

    lax.fori_loop(1, 64, wait_lat, 0)
    b.finish()


def exchange(lat, grads):
    in_vmem = pl.BlockSpec(memory_space=pltpu.VMEM)
    block = (48, 128)
    copies = 8 + 6 + 6 + 14
    return pl.pallas_call(
        exchange_kernel,
        out_shape=[jax.ShapeDtypeStruct((64, 32, 128), BF), jax.ShapeDtypeStruct((2, 48, 128), F32)],
        in_specs=[in_vmem] * 2,
        out_specs=[in_vmem] * 2,
        scratch_shapes=[
            pltpu.VMEM((2, 4, 2, 4, 4) + block, BF),
            pltpu.VMEM((2, 4, 2, 4, 4) + block, BF),
            pltpu.VMEM((2, 3, 2, 4, 4) + block, BF),
            pltpu.VMEM((2, 4, 2, 4) + block, BF),
            pltpu.VMEM((2, 3, 2, 4) + block, BF),
            pltpu.VMEM((2, 2, 4) + block, BF),
            pltpu.VMEM((2, 7) + block, BF),
            pltpu.SemaphoreType.DMA((2, 63)),
            pltpu.SemaphoreType.DMA,
            pltpu.SemaphoreType.DMA((copies,)),
            pltpu.SemaphoreType.DMA((copies,)),
        ],
        compiler_params=pltpu.CompilerParams(collective_id=1, has_side_effects=True, vmem_limit_bytes=VMEM_LIMIT),
        name="exchange",
    )(lat, grads.reshape((2, 4, 4, 2, 4, 2) + block))


def on_device(
    student_tiles, teacher_tiles, send_list, clip_weight, kernel_dilated, kernel_mix, kernel_down, kernel_proj,
    kernel_teacher, alpha_one, alpha_two, alpha_three, alpha_teacher,
):
    teach, down, proj, dil, mix, cw = gather_kernels(
        kernel_teacher, kernel_down, kernel_proj, kernel_dilated, kernel_mix, clip_weight
    )
    gathered = (
        teach.reshape(4, 16, 128, 1024), down.reshape(4096, 512), proj.reshape(512, 1024),
        dil.reshape(1792, 256), mix.reshape(256, 256),
    )
    d = lax.axis_index("dp")
    routes = send_list.reshape(64, 2).T.reshape(128, 1)
    weight = lax.dynamic_slice(cw.reshape(64, 128), (0, 2 * d), (64, 2)).T.reshape(128, 1)
    lat, grads = local_step(
        routes,
        jnp.concatenate([weight, weight], axis=0),
        student_tiles.reshape(2048, 256),
        teacher_tiles.reshape(2048, 512),
        gathered,
        [a.reshape(1, -1) for a in (alpha_one, alpha_two, alpha_three, alpha_teacher)],
    )
    lat, total = exchange(lat, grads)
    total = total.reshape(96, 128)
    g_down = total[0:64].reshape(4, 16, 128).transpose(1, 0, 2).reshape(-1)
    return (
        lat.reshape(128, 2, 1024),
        total[64:80][0:14].reshape(-1),
        total[78:80].reshape(-1),
        g_down,
        total[80:96].reshape(-1),
    )


def solution(mesh):
    both = P(("dp", "fsdp"))
    return jax.shard_map(
        on_device,
        mesh=mesh,
        in_specs=(
            P(("dp", "fsdp"), None, None),
            P(("dp", "fsdp"), None, None),
            P("dp", "fsdp", None),
            both,
            P("fsdp", None),
            P("fsdp", None),
            P("fsdp", None),
            P("fsdp", None),
            P(None, "fsdp", None),
            P(),
            P(),
            P(),
            P(),
        ),
        out_specs=(P(("dp", "fsdp"), None, None), both, both, both, both),
        check_vma=False,
    )
```

time: 769 us -> 208 us (0.27); the launches traced: 759 us -> 208 us
  waiting for transfers between devices: 336 us -> 0 us
  Pallas kernels: 0 us -> 195 us
  blocking collectives: 184 us -> 0 us
  local copies, waits for them, and re-layouts: 92.4 us -> 10.5 us
  matrix products: 61.1 us -> 0 us
  other arithmetic: 45.3 us -> 1.32 us
  starting transfers between devices: 26.6 us -> 0 us
  between operations: 14.5 us -> 0.68 us
    unnamed x5 -> x0, waiting for transfers between devices: 289 us -> none
    pallas_call x0 -> x3, Pallas kernels: none -> 195 us  [the longest x1 91 us: gather_kernels(): pl.pallas_call(gather_kernel, out_shape=outs, in_specs=[anywhere] * 6, ou...]
    all_to_all x1 -> x0, blocking collectives: 93.7 us -> none  [teacher_forward(): lax.all_to_all(activated, 'fsdp', split_axis=2, concat_axis=0, tiled=True)]
    all_gather x2 -> x0, blocking collectives: 90 us -> none  [the longest x1 56 us: on_device(): lax.all_gather(kernel_mix, 'fsdp', axis=0, tiled=True)]
    dot_general x11 -> x0, matrix products: 61.1 us -> none  [the longest x1 15.2 us: student_step(): jnp.dot(act_two, kernel_mix, preferred_element_type=jnp.float32)]
    all_to_all x2 -> x0, waiting for transfers between devices: 46.7 us -> none  [the longest x1 46.7 us: on_device(): lax.all_to_all(packed(teacher_tiles), 'dp', split_axis=0, concat_axis=0,...]
    unnamed x53 -> x2, local copies, waits for them, and re-layouts: 39.3 us -> 0.58 us
    convert_element_type x4 -> x0, other arithmetic: 30.8 us -> none  [the longest x1 15 us: teacher_forward(): activated = snake(tiles, alpha_teacher).astype(jnp.bfloat16)]
  transfers between devices with their start and end apart: 6 -> 0, of which waited for: 2 -> 0; matrix products, arithmetic and copies ran while one was open for 17% -> 0% of each run, Pallas kernels for 0% -> 0%
where the time goes in v1:
time: 208 us
  Pallas kernels  195 us (94%)
  local copies, waits for them, and re-layouts  10.5 us (5%)
    pallas_call x1, Pallas kernels, gather_kernels(): pl.pallas_call(gather_kernel, out_shape=outs, in_specs=[anywhere] * 6, ou...  91 us
    pallas_call x1, Pallas kernels, exchange(): pl.pallas_call(exchange_kernel, out_shape=[jax.ShapeDtypeStruct((64, 32,...  55 us
    pallas_call x1, Pallas kernels, local_step(): pl.pallas_call(step_kernel, out_shape=[jax.ShapeDtypeStruct((64, 32, 128)...  49 us

profile of v1, /device:TPU:8, one launch (start us, length us, event | category | flops | bytes accessed | tf_op | source)
XLA Modules:
  0.0 207.5 jit_solution(4969813235610662006)
XLA Ops:
  0.6 0.5 broadcast.3
  1.1 1.3 reduce.3
  2.5 0.1 reshape.97
  2.6 0.1 copy.38
  2.7 0.8 reshape.126.routes
  3.5 91.0 %gather_kernels.1 = (bf16[4,4,4,2,2,2,16,1024]{7,6,5,4,3,2,1,0:T(8,128)(2,1)}, bf16[4,4,4,2,2,16,512]{6,5,4,3,2,1,0:T(8,128)(2,1)}, bf16[4,2,64,1024]{3,2,1,0:T(...) custom-call(bf16[4,4,2,2,2,16,1024]{6,5,4,3,2,1,0:T(8,128)(2,1)} %bi, ...), custom_call_target="tpu_custom_call" | custom-call | tf_op jit(solution)/shard_map/gather_kernels/pallas_call | solution.py:268
  94.4 0.8 constant_dynamic-slice_fusion
  95.3 0.1 copy.43
  95.4 0.1 reshape.106
  95.4 0.8 copy.41.weight
  96.3 49.0 %local_step.1 = (bf16[64,32,128]{2,1,0:T(8,128)(2,1)}, bf16[256,96,128]{2,1,0:T(8,128)(2,1)}) custom-call(s32[128,1]{1,0:T(8,128)} %reshape.126.routes, f32[256,1]{1,0:T(8,128)} %copy.41.weight, bf16[2048,256]{1,0:T(8,128)(2,1)} %bitcast.37, bf16[2048,512]{1,0:T(8,128)(2,1)} %bitcast.36, bf16[4,16,128,1024]{3,2,1,0:T(8,128)(2,1)} %bitcast.32, ...), custom_call_target="tpu_custom_call" | custom-call | tf_op jit(solution)/shard_map/local_step/pallas_call | solution.py:465
  145.3 55.0 %exchange.1 = (bf16[64,32,128]{2,1,0:T(8,128)(2,1)}, f32[2,48,128]{2,1,0:T(8,128)}) custom-call(bf16[64,32,128]{2,1,0:T(8,128)(2,1)} %get-tuple-element.21.lat, bf16[2,4,4,2,4,2,48,128]{7,6,5,4,3,2,1,0:T(8,128)(2,1)} %bitcast.33), custom_call_target="tpu_custom_call" | custom-call | tf_op jit(solution)/shard_map/exchange/pallas_call | solution.py:602
  200.3 2.0 reshape.119
  202.3 1.2 slice_bitcast_fusion.2
  203.5 1.3 slice_bitcast_fusion
  204.8 1.3 slice_bitcast_fusion.1
  206.1 0.8 slice.20
  206.9 0.6 copy.42
  (1 shorter events, 0.0 us)

commit v2 on v1

v2 whole, which is shorter than its diff:
```python
import jax
import jax.numpy as jnp
import numpy as np
from jax import lax
from jax.experimental import pallas as pl
from jax.experimental.pallas import tpu as pltpu
from jax.sharding import PartitionSpec as P

BF = jnp.bfloat16
F32 = jnp.float32
MESH = pl.DeviceIdType.MESH
VMEM_LIMIT = 66_000_000


def dot(a, b):
    return jnp.dot(a, b, preferred_element_type=F32)


def dot_bt(a, b):
    return lax.dot_general(a, b, (((1,), (1,)), ((), ())), preferred_element_type=F32)


PI_PARTS = (3.125, 0.015625, 9.67502593994140625e-4, 1.509957990978376432e-7)


def fit_sin_cos():
    nodes = np.cos(np.pi * (np.arange(400) + 0.5) / 400)
    u = (nodes + 1) * 0.5 * (np.pi / 2 * 1.002) ** 2
    r = np.sqrt(u)
    sin_c = np.polynomial.polynomial.polyfit(u, np.sin(r) / r, 5)
    cos_c = np.polynomial.polynomial.polyfit(u, np.cos(r), 5)
    return [float(c) for c in sin_c], [float(c) for c in cos_c]


SIN_C, COS_C = fit_sin_cos()


def horner(u, coefs):
    acc = jnp.full_like(u, coefs[-1])
    for c in coefs[-2::-1]:
        acc = acc * u + c
    return acc


def reduce_pi(y):
    n = jnp.round(y * (1.0 / np.pi))
    r = y
    for part in PI_PARTS:
        r = r - n * part
    return r


def snake_only(v, alpha, inv):
    r = reduce_pi(alpha * v)
    s = r * horner(r * r, SIN_C)
    return v + s * s * inv


def snake_slope(v, alpha, inv):
    r = reduce_pi(alpha * v)
    u = r * r
    s = r * horner(u, SIN_C)
    c = horner(u, COS_C)
    return v + s * s * inv, 1.0 + 2.0 * s * c


def coords():
    d = lax.axis_index("dp")
    f = lax.axis_index("fsdp")
    core = d % 2
    y = (d // 2) % 4
    x = (d // 8) % 4
    zhi = d // 32
    return d, f, zhi, x, y, core


def dp_of(zhi, x, y, core):
    return ((zhi * 4 + x) * 4 + y) * 2 + core


def z_peer(zhi, f, step):
    z = (zhi * 4 + f + step + 8) % 8
    return z // 4, z % 4


class Batch:
    def __init__(self, send, recv):
        self.send, self.recv, self.next = send, recv, 0
        self.all = []

    def start(self, src, dst, device):
        copy = pltpu.make_async_remote_copy(
            src_ref=src,
            dst_ref=dst,
            send_sem=self.send.at[self.next],
            recv_sem=self.recv.at[self.next],
            device_id=device,
            device_id_type=MESH,
        )
        self.next += 1
        copy.start()
        self.all.append(copy)
        return copy

    def finish(self):
        for copy in self.all:
            copy.wait_send()


GROUPS = ((0, 3), (3, 3), (6, 1), (7, 2), (9, 1), (10, 3), (13, 3))


def permutations():
    out = np.arange(256)
    tile = np.zeros((256, 256), np.float32)
    tile[out, (out % 16) * 16 + out // 16] = 1
    proj = np.zeros((256, 256), np.float32)
    block, m = out // 16, out % 16
    proj[out, (m % 8) * 32 + block * 2 + m // 8] = 1
    dil = np.zeros((256, 256), np.float32)
    dil[out, np.where(m < 14, (m % 2) * 112 + block * 7 + m // 2, 224 + (m - 14) * 16 + block)] = 1
    out = np.arange(512)
    lat = np.zeros((512, 512), np.float32)
    lat[out, (out % 32) * 16 + out // 32] = 1
    return [jnp.asarray(p, BF) for p in (tile, proj, dil, lat)]


EVERY = slice(None)
N_COPIES = 260


class Chunk:
    def __init__(self, batch, place, remote, peers, number, source, view):
        self.b, self.place, self.remote, self.number = batch, place, remote, number
        self.source, self.view = source, view
        self.peers = peers

    def start(self, own, z_peers):
        x, y = self.place
        self.z = [self.b.start(self.source, self.view(own, x, y, EVERY), peer) for peer in z_peers]

    def line(self, shard, along, step, wide, cut=EVERY):
        x, y = self.place
        half = along if not wide else 1 - along
        if along == 0:
            return self.view(shard, (x + step) % 4, cut if wide else y, half)
        return self.view(shard, cut if wide else x, (y + step) % 4, half)

    def z_done(self):
        for copy in self.z:
            copy.wait_recv()
        self.direct = []
        for along in (0, 1):
            for shard in self.remote:
                ref = self.line(shard, along, 0, False)
                for step in (1, -1):
                    self.direct.append(self.b.start(ref, ref, self.peers[along][step]))

    def first_relay(self):
        for copy in self.direct:
            copy.wait_recv()
        self.relay = []
        for along in (0, 1):
            for i, shard in enumerate(self.remote):
                step = 1 if (self.number + i + along) % 2 == 0 else -1
                ref = self.line(shard, along, -step, False)
                self.relay.append(self.b.start(ref, ref, self.peers[along][step]))

    def first_done(self):
        for copy in self.relay:
            copy.wait_recv()
        self.direct = []
        for along in (0, 1):
            for shard in self.remote:
                ref = self.line(shard, along, 0, True)
                for step in (1, -1):
                    self.direct.append(self.b.start(ref, ref, self.peers[along][step]))

    def second_relay(self):
        for copy in self.direct:
            copy.wait_recv()
        self.relay = []
        for along in (0, 1):
            for shard in self.remote:
                for step, cut in ((1, slice(0, 2)), (-1, slice(2, 4))):
                    ref = self.line(shard, along, -step, True, cut)
                    self.relay.append(self.b.start(ref, ref, self.peers[along][step]))

    def second_done(self):
        for copy in self.relay:
            copy.wait_recv()


def whole_kernel(
    teach_in, down_in, proj_in, dil_in, mix_in, cw_in, routes, xs, xt, a1, a2, a3, at, p_tile, p_proj, p_dil, p_lat,
    lat_g, total,
    w_t, w_d, w_p, w_l, w_m, cw, x1s, x1t, act1, act1t, act2t, act3, act3t, act_t, act_p, hid, slope3,
    tacc, tsend, targ, pred, error, back3, back_h, g_dil, stud, lat, grads, r0, s1, r1, s2, r2, s3, r3,
    local_sem, lat_sem, own_sem, send, recv,
):
    d, f, zhi, x, y, core = coords()
    partner = (dp_of(zhi, x, y, 1 - core), f)
    x_peers = [(dp_of(zhi, (x + k) % 4, y, core), f) for k in (1, 2, 3)]
    y_peers = [(dp_of(zhi, x, (y + k) % 4, core), f) for k in (1, 2, 3)]
    z_ids = [z_peer(zhi, f, k) for k in range(1, 8)]
    z_all = [(dp_of(h, x, y, core), g) for h, g in z_ids]
    far_h, far_f = z_peer(zhi, f, 2 - 4 * core)
    z_near = [z_all[0], z_all[6], (dp_of(far_h, x, y, core), far_f)]
    other = z_all[3]
    remote = [(f + r) % 4 for r in (1, 2, 3)]

    def columns(c):
        return pl.ds(pl.multiple_of(core * 512 + c * 256, 256), 256)

    loads = [
        (dil_in, w_l.at[f]), (mix_in, w_m.at[f]), (down_in, w_d.at[f]), (proj_in, w_p.at[f]),
        (cw_in, cw.at[zhi, x, y, core]),
    ]
    loads += [(teach_in.at[:, :, :, :, columns(c)], w_t.at[c, f]) for c in (0, 1)]
    loads = [pltpu.make_async_copy(src, dst, local_sem.at[i]) for i, (src, dst) in enumerate(loads)]
    for copy in loads:
        copy.start()

    barrier = pltpu.get_barrier_semaphore()
    for k, peer in enumerate(z_all):
        if k != 3:
            pl.semaphore_signal(barrier, inc=1, device_id=peer, device_id_type=MESH)

    def hello(k, carry):
        pl.semaphore_signal(barrier, inc=1, device_id=((d + k) % 64, f), device_id_type=MESH)
        return carry

    lax.fori_loop(1, 64, hello, 0)
    pl.semaphore_wait(barrier, 63 + 6)

    b = Batch(send, recv)
    peers = ({1: x_peers[0], -1: x_peers[2]}, {1: y_peers[0], -1: y_peers[2]})
    small = []
    for peer in z_near:
        small.append(b.start(dil_in.at[core], w_l.at[f, core], peer))
        small.append(b.start(mix_in.at[core], w_m.at[f, core], peer))
    cw_wait = [b.start(cw_in, cw.at[zhi, x, y, core], other)]
    cd = Chunk(b, (x, y), remote, peers, 0, down_in.at[x, y, core], lambda s, i, j, h: w_d.at[s, i, j, core, h])
    c0 = Chunk(
        b, (x, y), remote, peers, 1, teach_in.at[x, y, :, :, columns(0)], lambda s, i, j, h: w_t.at[0, s, i, j, h]
    )
    c1 = Chunk(
        b, (x, y), remote, peers, 0, teach_in.at[x, y, :, :, columns(1)], lambda s, i, j, h: w_t.at[1, s, i, j, h]
    )
    for chunk in (cd, c0, c1):
        chunk.start(f, z_near)
    small_p = [b.start(proj_in.at[core], w_p.at[f, core], peer) for peer in z_near]

    def alphas(ref):
        a = ref[...]
        return a, 1.0 / a

    @pl.loop(0, 8)
    def _(g):
        rows = pl.ds(pl.multiple_of(g * 256, 256), 256)
        cols = pl.ds(pl.multiple_of(g * 16, 16), 16)
        x1s[:, cols, :] = dot(p_tile[...], xs[rows, :]).astype(BF).reshape(16, 16, 256)
        x1t[:, cols, :] = dot(p_tile[...], xt[rows, :]).astype(BF).reshape(16, 16, 512)

    pick = jnp.where(
        routes[...] == lax.broadcasted_iota(jnp.int32, (128, 128), 1), 1.0, 0.0
    ).astype(BF)

    def teacher_act(low, high):
        @pl.loop(low, high)
        def _(j):
            act_t[j] = snake_only(dot(pick, x1t[j]), *alphas(at)).astype(BF)

    for chunk in (cd, c0, c1):
        chunk.z_done()
    for copy in small:
        copy.wait_recv()
    to_partner = []
    for shard in remote:
        to_partner.append(b.start(w_l.at[shard, core], w_l.at[shard, core], partner))
        to_partner.append(b.start(w_m.at[shard, core], w_m.at[shard, core], partner))
    loads[4].wait()
    for copy in cw_wait:
        copy.wait_recv()
    block = cw.at[:, x, y, core]
    cw_wait = [b.start(block, block, peer) for peer in x_peers]
    teacher_act(0, 8)
    for chunk in (cd, c0, c1):
        chunk.first_relay()
    teacher_act(8, 16)
    act_copy = b.start(act_t, act_p, partner)
    cd.first_done()
    c0.first_done()
    for copy in cw_wait:
        copy.wait_recv()
    block = cw.at[:, :, y, core]
    cw_wait = [b.start(block, block, peer) for peer in y_peers]
    for copy in small_p:
        copy.wait_recv()
    proj_copies = [b.start(w_p.at[shard, core], w_p.at[shard, core], partner) for shard in remote]
    c1.first_done()

    @pl.loop(0, 16)
    def _(j):
        value = dot(pick, x1s[j])
        x1s[j] = value.astype(BF)
        one = snake_only(value, *alphas(a1))
        act1[j] = one.astype(BF)
        act1t[j] = one.T.astype(BF)

    cd.second_relay()
    for copy in loads[0:2] :
        copy.wait()
    for copy in to_partner:
        copy.wait_recv()
    c0.second_relay()

    w_dil = w_l[...].reshape(1792, 256)
    for first, count in GROUPS:
        valid = [k for k in range(7) if 0 <= first + 3 * (k - 3) <= 15]
        lhs = jnp.concatenate(
            [act1[first + 3 * (k - 3) : first + 3 * (k - 3) + count].reshape(count * 128, 256) for k in valid], axis=1
        )
        hid[first : first + count] = dot(lhs, w_dil[valid[0] * 256 : (valid[-1] + 1) * 256, :]).reshape(count, 128, 256)
    cd.second_done()
    down_copies = [b.start(w_d.at[shard, :, :, core], w_d.at[shard, :, :, core], partner) for shard in remote]
    for copy in cw_wait:
        copy.wait_recv()
    block = cw.at[:, :, :, core]
    cw_wait = [b.start(block, block, partner)]

    @pl.loop(0, 16)
    def _(j):
        act, slope = snake_slope(hid[j], *alphas(a2))
        hid[j] = slope
        act2t[j] = act.T.astype(BF)
        residual = x1s[j].astype(F32) + dot(act.astype(BF), w_m[...].reshape(256, 256))
        act, slope = snake_slope(residual, *alphas(a3))
        slope3[j] = slope
        act3[j] = act.astype(BF)
        act3t[j] = act.T.astype(BF)

    c1.second_relay()

    for copy in down_copies + proj_copies:
        copy.wait_recv()
    for copy in loads[2:4]:
        copy.wait()

    def tap_rows(k):
        return w_d[k // 4, k % 4].reshape(256, 512)

    def shard_rows(s):
        return w_d[s].reshape(1024, 512)

    lhs = jnp.concatenate([jnp.concatenate([act3[k - 4], act3[k + 4]], axis=0) for k in range(4, 12)], axis=1)
    both = dot(lhs, w_d[1:3].reshape(2048, 512))
    first = dot(jnp.concatenate([act3[k] for k in range(8, 12)], axis=1), shard_rows(3))
    second = dot(jnp.concatenate([act3[k] for k in range(4, 8)], axis=1), shard_rows(0))
    stud[0:128, :] = (both[0:128] + first).astype(BF)
    stud[128:256, :] = (both[128:256] + second).astype(BF)
    w_proj = w_p[...].reshape(512, 1024)
    pred[...] = dot(stud[...], w_proj)

    @pl.loop(0, 4)
    def _(g):
        parts = [
            pred[pl.ds(pl.multiple_of(o * 128 + c * 64 + g * 16, 16), 16), cb * 128 : (cb + 1) * 128].astype(BF)
            for c in range(2)
            for o in range(2)
            for cb in range(8)
        ]
        moved = dot(p_lat[...], jnp.concatenate(parts, axis=0)).astype(BF)
        lat[pl.ds(g * 16, 16)] = moved.reshape(16, 32, 128)

    act_copy.wait_recv()
    target_copies = []
    for c, chunk in ((0, c0), (1, c1)):
        chunk.second_done()
        loads[5 + c].wait()
        tacc[...] = jnp.zeros_like(tacc)

        @pl.loop(4, 12)
        def _(k):
            lhs = jnp.concatenate([act_t[k - 4], act_p[k - 4], act_t[k + 4], act_p[k + 4]], axis=0)
            tacc[...] += dot(lhs, w_t[c, :, k // 4, k % 4].reshape(512, 256))

        @pl.loop(0, 4)
        def _(k):
            lhs = jnp.concatenate([act_t[k + 4], act_p[k + 4]], axis=0)
            tacc[256:512, :] += dot(lhs, w_t[c, :, 0, k].reshape(512, 256))
            lhs = jnp.concatenate([act_t[k + 8], act_p[k + 8]], axis=0)
            tacc[0:256, :] += dot(lhs, w_t[c, :, 3, k].reshape(512, 256))

        tsend[c, 0:128] = tacc[128:256, :].astype(BF)
        tsend[c, 128:256] = tacc[384:512, :].astype(BF)
        targ[core, c, 0:128] = tacc[0:128, :].astype(BF)
        targ[core, c, 128:256] = tacc[256:384, :].astype(BF)
        target_copies.append(b.start(tsend.at[c], targ.at[core, c], partner))

    own = pltpu.make_async_copy(lat.at[d], lat_g.at[d], own_sem)
    own.start()

    def lat_copy(k):
        to = (d + k) % 64
        return pltpu.make_async_remote_copy(
            src_ref=lat.at[to], dst_ref=lat_g.at[d], send_sem=lat_sem.at[0, k - 1], recv_sem=lat_sem.at[1, k - 1],
            device_id=(to, f), device_id_type=MESH,
        )

    def send_lat(k, carry):
        lat_copy(k).start()
        return carry

    lax.fori_loop(1, 64, send_lat, 0)

    for copy in cw_wait + target_copies:
        copy.wait_recv()
    lines = cw[...].reshape(64, 128)
    lane = lax.broadcasted_iota(jnp.int32, (64, 128), 1)
    pair = [jnp.sum(jnp.where(lane == 2 * d + c, lines, 0.0), axis=1, keepdims=True) for c in (0, 1)]
    weight = jnp.concatenate(pair + pair, axis=0)
    for cc in (0, 1):
        for c in (0, 1):
            cols = slice((cc * 2 + c) * 256, (cc * 2 + c + 1) * 256)
            error[:, cols] = (weight * (pred[:, cols] - targ[cc, c].astype(F32)) / 256.0).astype(BF)

    back_s = dot_bt(error[...], w_proj).astype(BF)

    def put(k, half, row, value):
        grads[k // 8, (k // 2) % 4, pl.ds((k % 2) * 2, 2), :, :, half, row : row + 16, :] = value.astype(BF).reshape(
            2, 2, 4, 16, 128
        )

    g_proj = dot(stud[...].astype(F32).T.astype(BF), error[...])
    pred[...] = g_proj[0:256]
    g_dil[0:1024, :] = jnp.concatenate([g_proj[256:512, i * 256 : (i + 1) * 256] for i in range(4)], axis=0)

    @pl.loop(0, 8)
    def _(g):
        low = [pred[pl.ds(pl.multiple_of(g * 32, 32), 32), i * 128 : (i + 1) * 128] for i in range(8)]
        high = [
            g_dil[pl.ds(pl.multiple_of((i // 2) * 256 + g * 32, 32), 32), (i % 2) * 128 : (i % 2 + 1) * 128]
            for i in range(8)
        ]
        for base, parts in ((0, low), (8, high)):
            put(base + g, 1, 32, dot(p_proj[...], jnp.concatenate(parts, axis=0).astype(BF)))

    stud[...] = back_s

    def put_down(k, value):
        for cb in range(4):
            put(k, cb // 3, (cb % 3) * 16, value[:, cb * 128 : (cb + 1) * 128])

    @pl.loop(4, 12)
    def _(k):
        put_down(k, dot(jnp.concatenate([act3t[k - 4], act3t[k + 4]], axis=1), stud[...]))
        part = dot_bt(stud[...], tap_rows(k))
        back3[k - 4] = part[0:128]
        back3[k + 4] = part[128:256]

    @pl.loop(0, 4)
    def _(k):
        put_down(k, dot(act3t[k + 4], stud[128:256, :]))
        put_down(k + 12, dot(act3t[k + 8], stud[0:128, :]))
        back3[k + 4] += dot_bt(stud[128:256, :], tap_rows(k))
        back3[k + 8] += dot_bt(stud[0:128, :], tap_rows(k + 12))

    order = (1, 2, 3, 0)
    pieces = [[], []]

    def to_core(h):
        for k in order:
            if h == 0:
                src = grads.at[:, (x + k) % 4, :, 1 - core, :, 0]
            else:
                src = grads.at[:, :, (y + k) % 4, 1 - core, :, 1]
            pieces[h].append(b.start(src, r0.at[h, k], partner))

    to_core(0)
    g_dil[1792:2048, :] = jnp.zeros((256, 256), F32)

    @pl.loop(0, 16)
    def _(j):
        back = (back3[j] * slope3[j]).astype(BF)
        g_dil[1792:2048, :] += dot(act2t[j], back)
        back_h[j] = (dot_bt(back, w_m[...].reshape(256, 256)) * hid[j]).astype(BF)

    first = [[], []]

    def sum_cores(h):
        for i, k in enumerate(order):
            pieces[h][i].wait_recv()

            @pl.loop(0, 8)
            def _(n):
                if h == 0:
                    mine = grads[n // 4, (x + k) % 4, n % 4, core, :, 0]
                else:
                    mine = grads[n // 4, n % 4, (y + k) % 4, core, :, 1]
                s1[h, k, n // 4, n % 4] = (mine.astype(F32) + r0[h, k, n // 4, n % 4].astype(F32)).astype(BF)

            if k > 0:
                first[h].append(b.start(s1.at[h, k], r1.at[h, k - 1], (x_peers, y_peers)[h][k - 1]))

    sum_cores(0)
    for k in range(7):
        shift = 3 * (k - 3)
        low, high = max(0, -shift), min(16, 16 - shift)
        lhs = jnp.concatenate([act1t[j + shift] for j in range(low, high)], axis=1)
        g_dil[k * 256 : (k + 1) * 256, :] = dot(lhs, back_h[low:high].reshape((high - low) * 128, 256))

    @pl.loop(0, 16)
    def _(g):
        rows = pl.ds(pl.multiple_of(g * 112, 16), 112)
        more = pl.ds(pl.multiple_of(1792 + g * 16, 16), 16)
        stack = jnp.concatenate(
            [g_dil[rows, 0:128], g_dil[rows, 128:256], g_dil[more, 0:128], g_dil[more, 128:256]], axis=0
        ).astype(BF)
        put(g, 1, 16, dot(p_dil[...], stack))

    to_core(1)
    sum_cores(1)

    second = [[], []]
    for h in (0, 1):
        for copy in first[h]:
            copy.wait_recv()

        @pl.loop(0, 8)
        def _(n):
            a, e = n // 4, n % 4
            acc = s1[h, 0, a, e].astype(F32)
            for k in range(3):
                acc = acc + r1[h, k, a, e].astype(F32)
            s2[h, e, a] = acc.astype(BF)

        mine = (y, x)[h]
        for k in (1, 2, 3):
            second[h].append(b.start(s2.at[h, (mine + k) % 4], r2.at[h, k - 1], (y_peers, x_peers)[h][k - 1]))
    third = [[], []]
    for h in (0, 1):
        for copy in second[h]:
            copy.wait_recv()
        mine = (y, x)[h]

        @pl.loop(0, 2)
        def _(a):
            acc = s2[h, mine, a].astype(F32)
            for k in range(3):
                acc = acc + r2[h, k, a].astype(F32)
            s3[h, a] = acc.astype(BF)

        for k in range(7):
            zh, zf = z_ids[k]
            third[h].append(b.start(s3.at[h, zh, zf], r3.at[h, k], z_all[k]))
    for h in (0, 1):
        for copy in third[h]:
            copy.wait_recv()
        acc = s3[h, zhi, f].astype(F32)
        for k in range(7):
            acc = acc + r3[h, k].astype(F32)
        total[h] = acc
    own.wait()

    def wait_lat(k, carry):
        copy = lat_copy(k)
        copy.wait_recv()
        copy.wait_send()
        return carry

    lax.fori_loop(1, 64, wait_lat, 0)
    b.finish()


def whole(teach, down, proj, dil, mix, clip_weight, routes, xs, xt, alphas):
    in_vmem = pl.BlockSpec(memory_space=pltpu.VMEM)
    anywhere = pl.BlockSpec(memory_space=pl.ANY)
    frames = lambda c, t: pltpu.VMEM((16, 128, c), t)
    turned = pltpu.VMEM((16, 256, 128), BF)
    block = (48, 128)
    args = [
        teach.reshape(4, 4, 2, 64, 1024),
        down.reshape(4, 4, 2, 2, 16, 512),
        proj.reshape(2, 64, 1024),
        dil.reshape(2, 224, 256),
        mix.reshape(2, 32, 256),
        clip_weight.reshape(1, 128),
    ]
    return pl.pallas_call(
        whole_kernel,
        out_shape=[jax.ShapeDtypeStruct((64, 32, 128), BF), jax.ShapeDtypeStruct((2,) + block, F32)],
        in_specs=[anywhere] * 6 + [in_vmem] * 11,
        out_specs=[in_vmem] * 2,
        scratch_shapes=[
            pltpu.VMEM((2, 4, 4, 4, 2, 64, 256), BF),
            pltpu.VMEM((4, 4, 4, 2, 2, 16, 512), BF),
            pltpu.VMEM((4, 2, 64, 1024), BF),
            pltpu.VMEM((4, 2, 224, 256), BF),
            pltpu.VMEM((4, 2, 32, 256), BF),
            pltpu.VMEM((2, 4, 4, 2, 1, 128), F32),
            frames(256, BF), frames(512, BF), frames(256, BF), turned, turned, frames(256, BF), turned,
            frames(512, BF), frames(512, BF), frames(256, F32), frames(256, F32),
            pltpu.VMEM((512, 256), F32), pltpu.VMEM((2, 256, 256), BF), pltpu.VMEM((2, 2, 256, 256), BF),
            pltpu.VMEM((256, 1024), F32), pltpu.VMEM((256, 1024), BF),
            frames(256, F32), frames(256, BF),
            pltpu.VMEM((2048, 256), F32), pltpu.VMEM((256, 512), BF),
            pltpu.VMEM((64, 32, 128), BF), pltpu.VMEM((2, 4, 4, 2, 4, 2) + block, BF),
            pltpu.VMEM((2, 4, 2, 4, 4) + block, BF),
            pltpu.VMEM((2, 4, 2, 4, 4) + block, BF),
            pltpu.VMEM((2, 3, 2, 4, 4) + block, BF),
            pltpu.VMEM((2, 4, 2, 4) + block, BF),
            pltpu.VMEM((2, 3, 2, 4) + block, BF),
            pltpu.VMEM((2, 2, 4) + block, BF),
            pltpu.VMEM((2, 7) + block, BF),
            pltpu.SemaphoreType.DMA((7,)),
            pltpu.SemaphoreType.DMA((2, 63)),
            pltpu.SemaphoreType.DMA,
            pltpu.SemaphoreType.DMA((N_COPIES,)),
            pltpu.SemaphoreType.DMA((N_COPIES,)),
        ],
        compiler_params=pltpu.CompilerParams(collective_id=0, has_side_effects=True, vmem_limit_bytes=VMEM_LIMIT),
        name="whole_step",
    )(*args, routes, xs, xt, *alphas, *permutations())


def on_device(
    student_tiles, teacher_tiles, send_list, clip_weight, kernel_dilated, kernel_mix, kernel_down, kernel_proj,
    kernel_teacher, alpha_one, alpha_two, alpha_three, alpha_teacher,
):
    routes = send_list.reshape(64, 2).T.reshape(128, 1)
    lat, total = whole(
        kernel_teacher, kernel_down, kernel_proj, kernel_dilated, kernel_mix, clip_weight,
        routes,
        student_tiles.reshape(2048, 256),
        teacher_tiles.reshape(2048, 512),
        [a.reshape(1, -1) for a in (alpha_one, alpha_two, alpha_three, alpha_teacher)],
    )
    total = total.reshape(96, 128)
    g_down = total[0:64].reshape(4, 16, 128).transpose(1, 0, 2).reshape(-1)
    return (
        lat.reshape(128, 2, 1024),
        total[64:78].reshape(-1),
        total[78:80].reshape(-1),
        g_down,
        total[80:96].reshape(-1),
    )


def solution(mesh):
    both = P(("dp", "fsdp"))
    return jax.shard_map(
        on_device,
        mesh=mesh,
        in_specs=(
            P(("dp", "fsdp"), None, None),
            P(("dp", "fsdp"), None, None),
            P("dp", "fsdp", None),
            both,
            P("fsdp", None),
            P("fsdp", None),
            P("fsdp", None),
            P("fsdp", None),
            P(None, "fsdp", None),
            P(),
            P(),
            P(),
            P(),
        ),
        out_specs=(P(("dp", "fsdp"), None, None), both, both, both, both),
        check_vma=False,
    )
```

time: 208 us -> 151 us (0.73)
  Pallas kernels: 195 us -> 139 us
    pallas_call x3 -> x1, Pallas kernels: 195 us -> 139 us  [whole(): pl.pallas_call(whole_kernel, out_shape=[jax.ShapeDtypeStruct((64, 32, 128...]
where the time goes in v2:
time: 151 us; the launch traced here: 150 us
  Pallas kernels  139 us (92%)
  local copies, waits for them, and re-layouts  8.68 us (6%)
    pallas_call x1, Pallas kernels, whole(): pl.pallas_call(whole_kernel, out_shape=[jax.ShapeDtypeStruct((64, 32, 128...  139 us

profile of v2, /device:TPU:8, one launch (start us, length us, event | category | flops | bytes accessed | tf_op | source)
XLA Modules:
  0.0 150.0 jit_solution(17016362567149749928)
XLA Ops:
  0.6 0.5 broadcast.3
  1.1 1.3 reduce.3
  2.5 0.1 reshape.79
  2.6 0.1 copy.26
  2.7 0.8 reshape.94.routes
  3.5 139.4 %whole_step.1 = (bf16[64,32,128]{2,1,0:T(8,128)(2,1)}, f32[2,48,128]{2,1,0:T(8,128)}) custom-call(bf16[4,4,2,64,1024]{4,3,2,1,0:T(8,128)(2,1)} %bitcast.24, bf16[4,4,2,2,16,512]{5,4,3,2,1,0:T(8,128)(2,1)} %bitcast.26, bf16[2,64,1024]{2,1,0:T(8,128)(2,1)} %bitcast.28, bf16[2,224,256]{2,1,0:T(8,128)(2,1)} %bitcast.29, bf16[2,32,256]{2,1,0:T(8,128)(2,1)} %bitcast.36, ...), custom_call_target="tpu_custom_call" | custom-call | tf_op jit(solution)/shard_map/whole_step/pallas_call | solution.py:590
  142.8 2.0 %reshape.87 = bf16[128,2,1024]{2,1,0:T(2,128)(2,1)} reshape(bf16[64,32,128]{2,1,0:T(8,128)(2,1)} %get-tuple-element.7) | data formatting | bytes 1048576 | tf_op jit(solution)/shard_map/reshape | solution.py:642
  144.8 1.2 slice_bitcast_fusion.2
  146.0 1.3 slice_bitcast_fusion
  147.3 1.3 slice_bitcast_fusion.1
  148.6 0.8 slice.18
  149.4 0.6 copy.28
